TPU v7x, 512 devices: a whole 4x8x8 slice. The times are simulated.
512 devices in a mesh: seq: 64 (over y, z), tensor: 8 (over x, core).
Axes of the slice: x: 4, y: 8, z: 8, core: 2. Of those that a mesh axis runs over, the one named last changes fastest.
Arguments:
- query_rows: bfloat16 [8192, 4096], P('seq', 'tensor'), may hold values from -6 to 6
- key_rows: bfloat16 [8192, 4096], P('seq', 'tensor'), may hold values from -6 to 6
- value_rows: bfloat16 [8192, 4096], P('seq', 'tensor'), may hold values from -6 to 6
- block_mask: int32 [64, 1], P('seq'), may hold values 0 or 1
- norm_gain: float32 [4096], P('tensor'), may hold values from 0.1 to 1.9
- out_weight: bfloat16 [4096, 4096], P('tensor'), may hold values from -0.125 to 0.125
Outputs:
- mixed: bfloat16 [8192, 4096], P('seq', 'tensor')
All inputs are finite; a program needn't handle non-finite values. No bound on the sum of `block_mask` on one device may be relied on, other than what follows from the above.
Results may differ from a plain program's by a relative error of at most 0.014.
Values may be sent and summed in bfloat16 or wider, within the bound.
A program may use at most 64 MiB of HBM per device.

v0:
```python
import jax
import jax.numpy as jnp
from jax import lax
from jax.sharding import PartitionSpec as P

DH = 128


def prefix_2(value, axis, join, neutral):
    count, mine = (lax.axis_size(axis), lax.axis_index(axis))
    pieces = lax.all_gather(value, axis)
    total = jnp.full_like(value, 0) + jnp.asarray(neutral, value.dtype)

    def turn(position, total):
        longer = join(total, pieces[position])
        return jnp.where(position < mine, longer, total)

    return lax.fori_loop(0, count - 1, turn, total)


def add_states(earlier, later):
    return earlier + later


def local(query_rows, key_rows, value_rows, block_mask, norm_gain, out_weight):
    tok_count = query_rows.shape[0]
    head_count = norm_gain.shape[0] // DH
    query_heads = query_rows.reshape(tok_count, head_count, DH)
    key_heads = key_rows.reshape(tok_count, head_count, DH)
    value_heads = value_rows.reshape(tok_count, head_count, DH)
    local_state = jnp.einsum(
        "thd,the->hde", key_heads, value_heads, preferred_element_type=jnp.float32
    )
    prefix = prefix_2(local_state, "seq", add_states, jnp.zeros_like(local_state))
    scores = jnp.einsum("thd,shd->hts", query_heads, key_heads, preferred_element_type=jnp.float32)
    blocks = block_mask.shape[0]
    block_len = tok_count // blocks
    expanded = jnp.broadcast_to(
        block_mask[:, None, :, None], (blocks, block_len, blocks, block_len)
    ).reshape(tok_count, tok_count)
    row_pos = lax.broadcasted_iota(jnp.int32, (tok_count, tok_count), 0)
    col_pos = lax.broadcasted_iota(jnp.int32, (tok_count, tok_count), 1)
    allowed = (expanded > 0) & (col_pos <= row_pos)
    weights = jnp.where(allowed[None], scores, 0.0).astype(jnp.bfloat16)
    intra = jnp.einsum("hts,she->the", weights, value_heads, preferred_element_type=jnp.float32)
    inter = jnp.einsum(
        "thd,hde->the", query_heads.astype(jnp.float32), prefix, precision=lax.Precision.HIGHEST
    )
    attn = intra + inter
    meansq = jnp.mean(attn * attn, axis=-1, keepdims=True)
    normed = attn * lax.rsqrt(meansq + 1e-05) * norm_gain.reshape(head_count, DH)
    gated = normed.reshape(tok_count, head_count * DH).astype(jnp.bfloat16)
    terms = jnp.dot(gated, out_weight, preferred_element_type=jnp.float32).astype(jnp.bfloat16)
    mixed = lax.psum_scatter(
        terms.astype(jnp.float32).astype(jnp.bfloat16), "tensor", scatter_dimension=1, tiled=True
    )
    return mixed


def solution(mesh):
    placed = (
        P("seq", "tensor"),
        P("seq", "tensor"),
        P("seq", "tensor"),
        P("seq", None),
        P("tensor"),
        P("tensor", None),
    )
    return jax.shard_map(
        local, mesh=mesh, in_specs=placed, out_specs=P("seq", "tensor"), check_vma=False
    )
```

profile of v0, /device:TPU:8, one launch (start us, length us, event | category | flops | bytes accessed | tf_op | source)
XLA Modules:
  0.0 268.8 jit_solution(18124311234143690749)
XLA Ops:
  6.5 1.1 copy.18
  7.6 1.8 fusion.3
  10.2 1.3 convolution_bitcast_fusion.1
  11.4 143.3 %all-gather.3.cloned.1.call-done = f32[256,128,128]{2,1,0:T(8,128)} async-done(((f32[4,128,128]{2,1,0:T(8,128)}), f32[256,128,128]{2,1,0:T(8,128)}) %all-gather.3.cloned.1.call-update) | async-done | bytes 16777232 | tf_op jit(solution)/shard_map/all_gather | solution.py:11
  154.7 67.1 %while.14 = (s32[]{:T(128)}, f32[4,128,128]{2,1,0:T(8,128)S(1)}, s32[]{:T(128)}, f32[64,4,128,128]{3,2,1,0:T(8,128)}, s32[]{:T(128)}, /*index=5*/s32[]{:T(128)}) while((s32[]{:T(128)}, f32[4,128,128]{2,1,0:T(8,128)S(1)}, s32[]{:T(128)}, f32[64,4,128,128]{3,2,1,0:T(8,128)}, s32[]{:T(128)}, /*index=5*/s32[]{:T(128)}) %tuple.40), condition=%wide.region_1.2_spmd.clone, body=%wide.region_0.1_spmd.clone.sunk | while | flops 196612 | bytes 786525 | solution.py:18
  155.7 1.0 add_select_fusion.2
  156.8 1.0 add_select_fusion.2
  157.9 1.0 add_select_fusion.2
  158.9 1.0 add_select_fusion.2
  160.0 1.0 add_select_fusion.2
  161.1 1.0 add_select_fusion.2
  162.1 1.0 add_select_fusion.2
  163.2 1.0 add_select_fusion.2
  164.3 1.0 add_select_fusion.2
  165.3 1.0 add_select_fusion.2
  166.4 1.0 add_select_fusion.2
  167.4 1.0 add_select_fusion.2
  168.5 1.0 add_select_fusion.2
  169.6 1.0 add_select_fusion.2
  170.6 1.0 add_select_fusion.2
  171.7 1.0 add_select_fusion.2
  172.8 1.0 add_select_fusion.2
  173.8 1.0 add_select_fusion.2
  174.9 1.0 add_select_fusion.2
  176.0 1.0 add_select_fusion.2
  177.0 1.0 add_select_fusion.2
  178.1 1.0 add_select_fusion.2
  179.2 1.0 add_select_fusion.2
  180.2 1.0 add_select_fusion.2
  181.3 1.0 add_select_fusion.2
  182.4 1.0 add_select_fusion.2
  183.4 1.0 add_select_fusion.2
  184.5 1.0 add_select_fusion.2
  185.5 1.0 add_select_fusion.2
  186.6 1.0 add_select_fusion.2
  187.7 1.0 add_select_fusion.2
  188.7 1.0 add_select_fusion.2
  189.8 1.0 add_select_fusion.2
  190.9 1.0 add_select_fusion.2
  191.9 1.0 add_select_fusion.2
  193.0 1.0 add_select_fusion.2
  194.1 1.0 add_select_fusion.2
  195.1 1.0 add_select_fusion.2
  196.2 1.0 add_select_fusion.2
  197.3 1.0 add_select_fusion.2
  198.3 1.0 add_select_fusion.2
  199.4 1.0 add_select_fusion.2
  200.5 1.0 add_select_fusion.2
  201.5 1.0 add_select_fusion.2
  202.6 1.0 add_select_fusion.2
  203.6 1.0 add_select_fusion.2
  204.7 1.0 add_select_fusion.2
  205.8 1.0 add_select_fusion.2
  206.8 1.0 add_select_fusion.2
  207.9 1.0 add_select_fusion.2
  209.0 1.0 add_select_fusion.2
  210.0 1.0 add_select_fusion.2
  211.1 1.0 add_select_fusion.2
  212.2 1.0 add_select_fusion.2
  213.2 1.0 add_select_fusion.2
  216.4 1.0 add_select_fusion.2
  217.5 1.0 add_select_fusion.2
  222.3 3.9 %convolution_convert_fusion = bf16[128,4096]{1,0:T(8,128)(2,1)} fusion(bf16[128,512]{0,1:T(8,128)(2,1)S(1)} %bitcast.50, bf16[512,4096]{1,0:T(8,128)(2,1)} %param.13), kind=kOutput, calls=%fused_computation.1 | convolution fusion | flops 537395200 | bytes 5373952 | tf_op jit(solution)/shard_map/dot_general | solution.py:53
  226.2 35.7 %reduce-scatter.2.cloned.1.call-done = bf16[128,512]{1,0:T(8,128)(2,1)} async-done(((bf16[128,4096]{1,0:T(8,128)(2,1)}), bf16[128,512]{1,0:T(8,128)(2,1)}) %reduce-scatter.2.cloned.1.call-update) | async-done | bytes 131088 | tf_op jit(solution)/shard_map/reduce_scatter | solution.py:54
  (19 shorter events, 6.9 us)
Async XLA Ops:
  6.5 3.6 %copy-start = (bf16[128,512]{1,0:T(8,128)(2,1)S(1)}, bf16[128,512]{1,0:T(8,128)(2,1)}, u32[]{:S(2)}) copy-start(bf16[128,512]{1,0:T(8,128)(2,1)} %param.8) | copy-start | bytes 393220
  6.5 215.6 %copy-start.1 = (f32[512]{0:T(512)S(1)}, f32[512]{0:T(512)}, u32[]{:S(2)}) copy-start(f32[512]{0:T(512)} %param.12) | copy-start | bytes 6148
  6.5 148.1 %all-gather.3.cloned.1.call-start = ((), (), s32[]{:S(2)}) async-start(), calls=%async_computation.2 | async-start | bytes 17039360 | tf_op jit(solution)/shard_map/all_gather | solution.py:11
  9.4 252.6 %reduce-scatter.2.cloned.1.call-start = ((), (), s32[]{:S(2)}) async-start(), calls=%async_computation.1 | async-start | bytes 1179648 | tf_op jit(solution)/shard_map/reduce_scatter | solution.py:54
Sparse Core Ops, SparseCore 0:
  10.3 144.2 all-gather.2
  226.4 35.5 reduce-scatter.1
where the time goes:
time: 271 us; the launch traced here: 269 us
  waiting for transfers between devices  179 us (66%)
  other arithmetic  65.7 us (24%)
  between operations  14.1 us (5%)
  matrix products  7.34 us (3%)
    all_gather x1, waiting for transfers between devices, prefix_2(): pieces = lax.all_gather(value, axis)  143 us
    select_n x63, other arithmetic, turn(): return jnp.where(position < mine, longer, total)  65.5 us
    reduce_scatter x1, waiting for transfers between devices, local(): lax.psum_scatter(terms.astype(jnp.float32).astype(jnp.bfloat16), 'tensor'...  35.7 us
  transfers between devices with their start and end apart: 2, of which 2 were waited for; matrix products, arithmetic and copies ran while one was open for 0% of the time, Pallas kernels for 0%

commit v1 on v0

v1 whole, which is shorter than its diff:
```python
import functools
import math

import jax
import jax.numpy as jnp
from jax import lax
from jax.experimental import pallas as pl
from jax.experimental.pallas import tpu as pltpu
from jax.sharding import PartitionSpec as P

DH = 128
F32, BF16 = jnp.float32, jnp.bfloat16
MESH = pl.DeviceIdType.MESH
PARTS = 2


def far_first(n):
    return sorted(range(1, n), key=lambda k: -min(k, n - k))


def kernel(ny, nz, nx, q_hbm, k_hbm, v_hbm, m_hbm, g_hbm, w_hbm, out_ref, q, k, v, m, g, w, state, rows, before, total,
           cols, ready, prefix, intra, gated, mine, pair_out, pair_in, chip_out, chip_in, load_sem, wload_sem, sa, ra, sb, rb,
           sc, rc, sp, rp, sx, rx):
    tok, feat = q.shape
    heads = feat // DH
    sl = DH // nz
    lw = feat // PARTS
    width = w.shape[2]
    seq, ten = lax.axis_index("seq"), lax.axis_index("tensor")
    y, z = seq // nz, lax.rem(seq, nz)
    x, c = ten // 2, lax.rem(ten, 2)

    def row_peer(j):
        pz = lax.rem(z + j, nz)
        return pz, (y * nz + pz, ten)

    def col_peer(j):
        py = lax.rem(y + j, ny)
        return py, (py * nz + z, ten)

    def chip_peer(j):
        px = lax.rem(x + j, nx)
        return px, (seq, px * 2 + c)

    partner = (seq, x * 2 + (1 - c))

    loads = [pltpu.make_async_copy(a, b, load_sem.at[i]) for i, (a, b) in enumerate(
        ((k_hbm, k), (v_hbm, v), (q_hbm, q), (m_hbm, m), (g_hbm, g)))]
    for copy in loads:
        copy.start()
    hops = far_first(nx) + [0]
    wloads = []
    for i, j in enumerate(hops):
        px, _ = chip_peer(j)
        for half, core in ((0, 1 - c), (1, c)):
            columns = pl.ds(pl.multiple_of((px * 2 + core) * width, width), width)
            copy = pltpu.make_async_copy(w_hbm.at[:, columns], w.at[2 * i + half], wload_sem.at[2 * i + half])
            copy.start()
            wloads.append(copy)

    cols[...] = jnp.zeros_like(cols)
    barrier = pltpu.get_barrier_semaphore()
    peers = [row_peer(j)[1] for j in far_first(nz)] + [col_peer(j)[1] for j in far_first(ny)]
    peers += [chip_peer(j)[1] for j in far_first(nx)] + [partner]
    for peer in peers:
        pl.semaphore_signal(barrier, inc=1, device_id=peer, device_id_type=MESH)

    loads[0].wait()
    loads[1].wait()
    for h in range(heads):
        one = lax.dot_general(k[:, h * DH:(h + 1) * DH], v[:, h * DH:(h + 1) * DH], (((0,), (0,)), ((), ())),
                              preferred_element_type=F32)
        part, at = divmod(h * DH, lw)
        state[part, :, :, at:at + DH] = one.astype(BF16).reshape(nz, sl, DH)
    pl.semaphore_wait(barrier, len(peers))

    sends = []

    def send(src, dst, send_sem, recv_sem, device):
        copy = pltpu.make_async_remote_copy(src_ref=src, dst_ref=dst, send_sem=send_sem, recv_sem=recv_sem, device_id=device,
                                            device_id_type=MESH)
        copy.start()
        return copy

    def arrived(dst, recv_sem, send_sem, device):
        pltpu.make_async_remote_copy(src_ref=dst, dst_ref=dst, send_sem=send_sem, recv_sem=recv_sem, device_id=device,
                                     device_id_type=MESH).wait_recv()

    for p in range(PARTS):
        for j in far_first(nz):
            pz, device = row_peer(j)
            sends.append(send(state.at[p, pz], rows.at[p, z], sa.at[p, j], ra.at[p, z], device))
    for p in range(PARTS):
        rows[p, z] = state[p, z]

    for copy in loads[2:]:
        copy.wait()
    row_pos = lax.broadcasted_iota(jnp.int32, (tok, tok), 0)
    col_pos = lax.broadcasted_iota(jnp.int32, (tok, tok), 1)
    allowed = (jnp.full((tok, tok), m[0, 0], jnp.int32) > 0) & (col_pos <= row_pos)
    for h in range(heads):
        at = slice(h * DH, (h + 1) * DH)
        scores = lax.dot_general(q[:, at], k[:, at], (((1,), (1,)), ((), ())), preferred_element_type=F32)
        weights = jnp.where(allowed, scores, 0.0).astype(BF16)
        intra[:, at] = jnp.dot(weights, v[:, at], preferred_element_type=F32)

    for p in range(PARTS):
        for j in far_first(nz)[::-1]:
            pz, device = row_peer(j)
            arrived(rows.at[p, pz], ra.at[p, pz], sa.at[p, j], device)
        run = jnp.zeros((sl, lw), F32)
        for i in range(nz):
            before[p, i] = run
            run = run + rows[p, i].astype(F32)
        total[p] = run.astype(BF16)
        for j in range(ny - 1, 0, -1):
            @pl.when(y + j < ny)
            def _():
                send(total.at[p], cols.at[p, y], sb.at[p, j], rb.at[p, y], ((y + j) * nz + z, ten))

    for p in range(PARTS):
        for j in range(1, ny):
            @pl.when(y - j >= 0)
            def _():
                arrived(cols.at[p, y - j], rb.at[p, y - j], sb.at[p, j], ((y - j) * nz + z, ten))
        base = jnp.zeros((sl, lw), F32)
        for i in range(ny):
            base = base + cols[p, i].astype(F32)
        for i in range(nz):
            ready[p, i] = (base + before[p, i]).astype(BF16)
        for j in far_first(nz):
            pz, device = row_peer(j)
            sends.append(send(ready.at[p, pz], prefix.at[p, z], sc.at[p, j], rc.at[p, z], device))
        prefix[p, z] = ready[p, z]

    for p in range(PARTS):
        for j in far_first(nz)[::-1]:
            pz, device = row_peer(j)
            arrived(prefix.at[p, pz], rc.at[p, pz], sc.at[p, j], device)
        for h in range(heads // PARTS):
            at = slice(p * lw + h * DH, p * lw + (h + 1) * DH)
            one = prefix[p, :, :, h * DH:(h + 1) * DH].reshape(DH, DH)
            attn = intra[:, at] + jnp.dot(q[:, at], one, preferred_element_type=F32)
            meansq = jnp.mean(attn * attn, axis=-1, keepdims=True)
            gated[:, at] = (attn * lax.rsqrt(meansq + 1e-05) * g[:, at]).astype(BF16)

    for i, j in enumerate(hops):
        wloads[2 * i].wait()
        pair_out[i] = jnp.dot(gated[...], w[2 * i], preferred_element_type=F32).astype(BF16)
        sends.append(send(pair_out.at[i], pair_in.at[i], sp.at[i], rp.at[i], partner))
        wloads[2 * i + 1].wait()
        mine[i] = jnp.dot(gated[...], w[2 * i + 1], preferred_element_type=F32)
    for i, j in enumerate(hops):
        arrived(pair_in.at[i], rp.at[i], sp.at[i], partner)
        if j:
            chip_out[i] = (mine[i] + pair_in[i].astype(F32)).astype(BF16)
            sends.append(send(chip_out.at[i], chip_in.at[i], sx.at[i], rx.at[i], chip_peer(j)[1]))
    result = mine[len(hops) - 1] + pair_in[len(hops) - 1].astype(F32)
    for i, j in enumerate(hops[:-1]):
        arrived(chip_in.at[i], rx.at[i], sx.at[i], chip_peer(j)[1])
        result = result + chip_in[i].astype(F32)
    out_ref[...] = result.astype(BF16)

    for copy in sends:
        copy.wait_send()
    for p in range(PARTS):
        for j in range(1, ny):
            @pl.when(y + j < ny)
            def _():
                pltpu.make_async_remote_copy(src_ref=total.at[p], dst_ref=cols.at[p, y], send_sem=sb.at[p, j],
                                             recv_sem=rb.at[p, y], device_id=((y + j) * nz + z, ten),
                                             device_id_type=MESH).wait_send()


def solution(mesh):
    n_seq, n_ten = mesh.shape["seq"], mesh.shape["tensor"]
    nz = math.isqrt(n_seq)
    ny, nx = n_seq // nz, n_ten // 2

    def local(query_rows, key_rows, value_rows, block_mask, norm_gain, out_weight):
        tok, feat = query_rows.shape
        width = out_weight.shape[1] // n_ten
        sl, lw = DH // nz, feat // PARTS
        dma = pltpu.SemaphoreType.DMA
        slices = pltpu.VMEM((PARTS, nz, sl, lw), BF16)
        return pl.pallas_call(
            functools.partial(kernel, ny, nz, nx),
            out_shape=jax.ShapeDtypeStruct((tok, width), BF16),
            in_specs=[pl.BlockSpec(memory_space=pl.ANY)] * 6,
            out_specs=pl.BlockSpec(memory_space=pltpu.VMEM),
            scratch_shapes=[
                pltpu.VMEM((tok, feat), BF16), pltpu.VMEM((tok, feat), BF16), pltpu.VMEM((tok, feat), BF16),
                pltpu.SMEM((1, 1), jnp.int32), pltpu.VMEM((1, feat), F32),
                pltpu.VMEM((2 * nx, feat, width), BF16),
                slices, slices, pltpu.VMEM((PARTS, nz, sl, lw), F32), pltpu.VMEM((PARTS, sl, lw), BF16),
                pltpu.VMEM((PARTS, ny, sl, lw), BF16), slices, slices,
                pltpu.VMEM((tok, feat), F32), pltpu.VMEM((tok, feat), BF16),
                pltpu.VMEM((nx, tok, width), F32), pltpu.VMEM((nx, tok, width), BF16), pltpu.VMEM((nx, tok, width), BF16),
                pltpu.VMEM((nx, tok, width), BF16), pltpu.VMEM((nx, tok, width), BF16),
                dma((5,)), dma((2 * nx,)), dma((PARTS, nz)), dma((PARTS, nz)), dma((PARTS, ny)), dma((PARTS, ny)),
                dma((PARTS, nz)), dma((PARTS, nz)), dma((nx,)), dma((nx,)), dma((nx,)), dma((nx,)),
            ],
            compiler_params=pltpu.CompilerParams(collective_id=0, has_side_effects=True),
        )(query_rows, key_rows, value_rows, block_mask, norm_gain.reshape(1, feat), out_weight)

    placed = (P("seq", "tensor"), P("seq", "tensor"), P("seq", "tensor"), P("seq", None), P("tensor"), P("tensor", None))
    return jax.shard_map(local, mesh=mesh, in_specs=placed, out_specs=P("seq", "tensor"), check_vma=False)
```

time: 271 us -> 41.6 us (0.15)
  the two profiles are of different devices: /device:TPU:8 before, /device:TPU:49 now
where the time goes in v1:
time: 41.6 us; the launch traced here: 41.5 us
  Pallas kernels  39.2 us (94%)
  local copies, waits for them, and re-layouts  1.57 us (4%)
  between operations  0.66 us (2%)
    pallas_call x1, Pallas kernels, local(): pl.pallas_call(functools.partial(kernel, ny, nz, nx), out_shape=jax.Shape...  39.2 us
    unnamed x1, local copies, waits for them, and re-layouts  1.57 us

profile of v1, /device:TPU:49, one launch (start us, length us, event | category | flops | bytes accessed | tf_op | source)
XLA Modules:
  0.0 41.5 jit_solution(565458502696001036)
XLA Ops:
  0.7 39.2 %shard_map.64 = bf16[128,512]{1,0:T(8,128)(2,1)} custom-call(bf16[128,512]{1,0:T(8,128)(2,1)} %q_hbm.1, bf16[128,512]{1,0:T(8,128)(2,1)} %k_hbm.1, bf16[128,512]{1,0:T(8,128)(2,1)} %v_hbm.1, s32[1,1]{1,0:T(1,128)S(6)} %copy.8.m_hbm, f32[1,512]{1,0:T(1,128)} %bitcast.1, bf16[512,4096]{1,0:T(8,128)(2,1)} %w_hbm.1), custom_call_target="tpu_custom_call" | custom-call | tf_op jit(solution)/shard_map/pallas_call | solution.py:186
  39.9 1.6 %copy.9 = bf16[128,512]{1,0:T(8,128)(2,1)} copy(bf16[128,512]{1,0:T(8,128)(2,1)} %shard_map.64) | data formatting | bytes 262144

commit v2 on v1

--- a/solution.py
+++ b/solution.py
@@ -18,14 +18,15 @@
     return sorted(range(1, n), key=lambda k: -min(k, n - k))
 
 
-def kernel(ny, nz, nx, q_hbm, k_hbm, v_hbm, m_hbm, g_hbm, w_hbm, out_ref, q, k, v, m, g, w, state, rows, before, total,
-           cols, ready, prefix, intra, gated, mine, pair_out, pair_in, chip_out, chip_in, load_sem, wload_sem, sa, ra, sb, rb,
-           sc, rc, sp, rp, sx, rx):
+def kernel(ny, nz, nx, q_hbm, k_hbm, v_hbm, m_hbm, g_hbm, w_hbm, out_ref, q, k, v, m, g, w, w_in, state, rows, before, total,
+           cols, ready, prefix, intra, gated, gated_in, relay_out, relay_in, chip_out, chip_in, load_sem, wload_sem, sa, ra, sb,
+           rb, sc, rc, sw, rw, sg, rg, sr, rr, sx, rx):
     tok, feat = q.shape
     heads = feat // DH
     sl = DH // nz
     lw = feat // PARTS
     width = w.shape[2]
+    half = width // 2
     seq, ten = lax.axis_index("seq"), lax.axis_index("tensor")
     y, z = seq // nz, lax.rem(seq, nz)
     x, c = ten // 2, lax.rem(ten, 2)
@@ -48,20 +49,21 @@
         ((k_hbm, k), (v_hbm, v), (q_hbm, q), (m_hbm, m), (g_hbm, g)))]
     for copy in loads:
         copy.start()
-    hops = far_first(nx) + [0]
-    wloads = []
-    for i, j in enumerate(hops):
-        px, _ = chip_peer(j)
-        for half, core in ((0, 1 - c), (1, c)):
-            columns = pl.ds(pl.multiple_of((px * 2 + core) * width, width), width)
-            copy = pltpu.make_async_copy(w_hbm.at[:, columns], w.at[2 * i + half], wload_sem.at[2 * i + half])
-            copy.start()
-            wloads.append(copy)
+    hops = (2, 1, nx - 1, 0)
+
+    def block(i, core):
+        px, _ = chip_peer(hops[i])
+        return w_hbm.at[:, pl.ds(pl.multiple_of((px * 2 + core) * width, width), width)]
+
+    wloads = [pltpu.make_async_copy(block(i, c), w.at[i], wload_sem.at[i]) for i in range(nx)]
+    for copy in wloads:
+        copy.start()
 
     cols[...] = jnp.zeros_like(cols)
     barrier = pltpu.get_barrier_semaphore()
     peers = [row_peer(j)[1] for j in far_first(nz)] + [col_peer(j)[1] for j in far_first(ny)]
-    peers += [chip_peer(j)[1] for j in far_first(nx)] + [partner]
+    ahead, behind = chip_peer(1)[1], chip_peer(nx - 1)[1]
+    peers += [ahead, behind, partner]
     for peer in peers:
         pl.semaphore_signal(barrier, inc=1, device_id=peer, device_id_type=MESH)
 
@@ -90,6 +92,8 @@
         for j in far_first(nz):
             pz, device = row_peer(j)
             sends.append(send(state.at[p, pz], rows.at[p, z], sa.at[p, j], ra.at[p, z], device))
+    for i in range(nx):
+        sends.append(send(block(i, 1 - c), w_in.at[i], sw.at[i], rw.at[i], partner))
     for p in range(PARTS):
         rows[p, z] = state[p, z]
 
@@ -143,23 +147,43 @@
             attn = intra[:, at] + jnp.dot(q[:, at], one, preferred_element_type=F32)
             meansq = jnp.mean(attn * attn, axis=-1, keepdims=True)
             gated[:, at] = (attn * lax.rsqrt(meansq + 1e-05) * g[:, at]).astype(BF16)
-
-    for i, j in enumerate(hops):
-        wloads[2 * i].wait()
-        pair_out[i] = jnp.dot(gated[...], w[2 * i], preferred_element_type=F32).astype(BF16)
-        sends.append(send(pair_out.at[i], pair_in.at[i], sp.at[i], rp.at[i], partner))
-        wloads[2 * i + 1].wait()
-        mine[i] = jnp.dot(gated[...], w[2 * i + 1], preferred_element_type=F32)
-    for i, j in enumerate(hops):
-        arrived(pair_in.at[i], rp.at[i], sp.at[i], partner)
-        if j:
-            chip_out[i] = (mine[i] + pair_in[i].astype(F32)).astype(BF16)
-            sends.append(send(chip_out.at[i], chip_in.at[i], sx.at[i], rx.at[i], chip_peer(j)[1]))
-    result = mine[len(hops) - 1] + pair_in[len(hops) - 1].astype(F32)
-    for i, j in enumerate(hops[:-1]):
-        arrived(chip_in.at[i], rx.at[i], sx.at[i], chip_peer(j)[1])
-        result = result + chip_in[i].astype(F32)
-    out_ref[...] = result.astype(BF16)
+        at = pl.ds(p * lw, lw)
+        sends.append(send(gated.at[:, at], gated_in.at[:, at], sg.at[p], rg.at[p], partner))
+
+    def partial(i, part):
+        at = slice(part * half, (part + 1) * half)
+        return (jnp.dot(gated[...], w[i, :, at], preferred_element_type=F32) +
+                jnp.dot(gated_in[...], w_in[i, :, at], preferred_element_type=F32))
+
+    def there(i):
+        wloads[i].wait()
+        arrived(w_in.at[i], rw.at[i], sw.at[i], partner)
+
+    there(0)
+    for p in range(PARTS):
+        at = pl.ds(p * lw, lw)
+        arrived(gated_in.at[:, at], rg.at[p], sg.at[p], partner)
+    both = (ahead, behind)
+    for d in range(2):
+        relay_out[d] = partial(0, d).astype(BF16)
+        sends.append(send(relay_out.at[d], relay_in.at[d], sr.at[d], rr.at[d], both[d]))
+    for d in range(2):
+        there(1 + d)
+        chip_out[d, 1 - d] = partial(1 + d, 1 - d).astype(BF16)
+        sends.append(send(chip_out.at[d, 1 - d], chip_in.at[d, 1 - d], sx.at[d, 1 - d], rx.at[d, 1 - d], both[d]))
+    for d in range(2):
+        term = partial(1 + d, d)
+        arrived(relay_in.at[d], rr.at[d], sr.at[d], both[1 - d])
+        chip_out[d, d] = (term + relay_in[d].astype(F32)).astype(BF16)
+        sends.append(send(chip_out.at[d, d], chip_in.at[d, d], sx.at[d, d], rx.at[d, d], both[d]))
+    there(3)
+    own = [partial(3, part) for part in range(2)]
+    for d in range(2):
+        arrived(chip_in.at[d, 1 - d], rx.at[d, 1 - d], sx.at[d, 1 - d], both[1 - d])
+        own[1 - d] = own[1 - d] + chip_in[d, 1 - d].astype(F32)
+    for d in range(2):
+        arrived(chip_in.at[d, d], rx.at[d, d], sx.at[d, d], both[1 - d])
+        out_ref[:, d * half:(d + 1) * half] = (own[d] + chip_in[d, d].astype(F32)).astype(BF16)
 
     for copy in sends:
         copy.wait_send()
@@ -191,14 +215,15 @@
             scratch_shapes=[
                 pltpu.VMEM((tok, feat), BF16), pltpu.VMEM((tok, feat), BF16), pltpu.VMEM((tok, feat), BF16),
                 pltpu.SMEM((1, 1), jnp.int32), pltpu.VMEM((1, feat), F32),
-                pltpu.VMEM((2 * nx, feat, width), BF16),
+                pltpu.VMEM((nx, feat, width), BF16), pltpu.VMEM((nx, feat, width), BF16),
                 slices, slices, pltpu.VMEM((PARTS, nz, sl, lw), F32), pltpu.VMEM((PARTS, sl, lw), BF16),
                 pltpu.VMEM((PARTS, ny, sl, lw), BF16), slices, slices,
-                pltpu.VMEM((tok, feat), F32), pltpu.VMEM((tok, feat), BF16),
-                pltpu.VMEM((nx, tok, width), F32), pltpu.VMEM((nx, tok, width), BF16), pltpu.VMEM((nx, tok, width), BF16),
-                pltpu.VMEM((nx, tok, width), BF16), pltpu.VMEM((nx, tok, width), BF16),
-                dma((5,)), dma((2 * nx,)), dma((PARTS, nz)), dma((PARTS, nz)), dma((PARTS, ny)), dma((PARTS, ny)),
-                dma((PARTS, nz)), dma((PARTS, nz)), dma((nx,)), dma((nx,)), dma((nx,)), dma((nx,)),
+                pltpu.VMEM((tok, feat), F32), pltpu.VMEM((tok, feat), BF16), pltpu.VMEM((tok, feat), BF16),
+                pltpu.VMEM((2, tok, width // 2), BF16), pltpu.VMEM((2, tok, width // 2), BF16),
+                pltpu.VMEM((2, 2, tok, width // 2), BF16), pltpu.VMEM((2, 2, tok, width // 2), BF16),
+                dma((5,)), dma((nx,)), dma((PARTS, nz)), dma((PARTS, nz)), dma((PARTS, ny)), dma((PARTS, ny)),
+                dma((PARTS, nz)), dma((PARTS, nz)), dma((nx,)), dma((nx,)), dma((PARTS,)), dma((PARTS,)),
+                dma((2,)), dma((2,)), dma((2, 2)), dma((2, 2)),
             ],
             compiler_params=pltpu.CompilerParams(collective_id=0, has_side_effects=True),
         )(query_rows, key_rows, value_rows, block_mask, norm_gain.reshape(1, feat), out_weight)

time: 41.6 us -> 39.5 us (0.950)
  the two profiles are of different devices: /device:TPU:49 before, /device:TPU:41 now
where the time goes in v2:
time: 39.5 us; the launch traced here: 39.4 us
  Pallas kernels  37.1 us (94%)
  local copies, waits for them, and re-layouts  1.57 us (4%)
  between operations  0.66 us (2%)
    pallas_call x1, Pallas kernels, local(): pl.pallas_call(functools.partial(kernel, ny, nz, nx), out_shape=jax.Shape...  37.1 us
    unnamed x1, local copies, waits for them, and re-layouts  1.57 us

profile of v2, /device:TPU:41, one launch (start us, length us, event | category | flops | bytes accessed | tf_op | source)
XLA Modules:
  0.0 39.4 jit_solution(5624113882538564379)
XLA Ops:
  0.7 37.1 %shard_map.64 = bf16[128,512]{1,0:T(8,128)(2,1)} custom-call(bf16[128,512]{1,0:T(8,128)(2,1)} %q_hbm.1, bf16[128,512]{1,0:T(8,128)(2,1)} %k_hbm.1, bf16[128,512]{1,0:T(8,128)(2,1)} %v_hbm.1, s32[1,1]{1,0:T(1,128)S(6)} %copy.8.m_hbm, f32[1,512]{1,0:T(1,128)} %bitcast.1, bf16[512,4096]{1,0:T(8,128)(2,1)} %w_hbm.1), custom_call_target="tpu_custom_call" | custom-call | tf_op jit(solution)/shard_map/pallas_call | solution.py:210
  37.8 1.6 %copy.9 = bf16[128,512]{1,0:T(8,128)(2,1)} copy(bf16[128,512]{1,0:T(8,128)(2,1)} %shard_map.64) | data formatting | bytes 262144

commit v3 on v2

--- a/solution.py
+++ b/solution.py
@@ -12,6 +12,7 @@
 F32, BF16 = jnp.float32, jnp.bfloat16
 MESH = pl.DeviceIdType.MESH
 PARTS = 2
+CHUNKS = 2
 
 
 def far_first(n):
@@ -19,8 +20,8 @@
 
 
 def kernel(ny, nz, nx, q_hbm, k_hbm, v_hbm, m_hbm, g_hbm, w_hbm, out_ref, q, k, v, m, g, w, w_in, state, rows, before, total,
-           cols, ready, prefix, intra, gated, gated_in, relay_out, relay_in, chip_out, chip_in, load_sem, wload_sem, sa, ra, sb,
-           rb, sc, rc, sw, rw, sg, rg, sr, rr, sx, rx):
+           cols, ready, prefix, intra, gated, gated_in, relay_out, relay_in, direct_out, direct_in, chip_out, chip_in,
+           load_sem, wload_sem, sa, ra, sb, rb, sc, rc, sw, rw, sg, rg, sr, rr, sd, rd, sx, rx):
     tok, feat = q.shape
     heads = feat // DH
     sl = DH // nz
@@ -45,20 +46,6 @@
 
     partner = (seq, x * 2 + (1 - c))
 
-    loads = [pltpu.make_async_copy(a, b, load_sem.at[i]) for i, (a, b) in enumerate(
-        ((k_hbm, k), (v_hbm, v), (q_hbm, q), (m_hbm, m), (g_hbm, g)))]
-    for copy in loads:
-        copy.start()
-    hops = (2, 1, nx - 1, 0)
-
-    def block(i, core):
-        px, _ = chip_peer(hops[i])
-        return w_hbm.at[:, pl.ds(pl.multiple_of((px * 2 + core) * width, width), width)]
-
-    wloads = [pltpu.make_async_copy(block(i, c), w.at[i], wload_sem.at[i]) for i in range(nx)]
-    for copy in wloads:
-        copy.start()
-
     cols[...] = jnp.zeros_like(cols)
     barrier = pltpu.get_barrier_semaphore()
     peers = [row_peer(j)[1] for j in far_first(nz)] + [col_peer(j)[1] for j in far_first(ny)]
@@ -66,6 +53,20 @@
     peers += [ahead, behind, partner]
     for peer in peers:
         pl.semaphore_signal(barrier, inc=1, device_id=peer, device_id_type=MESH)
+
+    loads = [pltpu.make_async_copy(a, b, load_sem.at[i]) for i, (a, b) in enumerate(
+        ((k_hbm, k), (v_hbm, v), (q_hbm, q), (m_hbm, m), (g_hbm, g)))]
+    for copy in loads:
+        copy.start()
+    hops = (2, 1, nx - 1, 0)
+
+    def block(i, core):
+        px, _ = chip_peer(hops[i])
+        return w_hbm.at[:, pl.ds(pl.multiple_of((px * 2 + core) * width, width), width)]
+
+    wloads = [pltpu.make_async_copy(block(i, c), w.at[i], wload_sem.at[i]) for i in range(nx)]
+    for copy in wloads:
+        copy.start()
 
     loads[0].wait()
     loads[1].wait()
@@ -117,7 +118,7 @@
             before[p, i] = run
             run = run + rows[p, i].astype(F32)
         total[p] = run.astype(BF16)
-        for j in range(ny - 1, 0, -1):
+        for j in far_first(ny):
             @pl.when(y + j < ny)
             def _():
                 send(total.at[p], cols.at[p, y], sb.at[p, j], rb.at[p, y], ((y + j) * nz + z, ten))
@@ -150,40 +151,51 @@
         at = pl.ds(p * lw, lw)
         sends.append(send(gated.at[:, at], gated_in.at[:, at], sg.at[p], rg.at[p], partner))
 
+    def product(features, weights, i, part):
+        return jnp.dot(features[...], weights[i, :, part * half:(part + 1) * half], preferred_element_type=F32)
+
     def partial(i, part):
-        at = slice(part * half, (part + 1) * half)
-        return (jnp.dot(gated[...], w[i, :, at], preferred_element_type=F32) +
-                jnp.dot(gated_in[...], w_in[i, :, at], preferred_element_type=F32))
+        return product(gated, w, i, part) + product(gated_in, w_in, i, part)
 
     def there(i):
         wloads[i].wait()
         arrived(w_in.at[i], rw.at[i], sw.at[i], partner)
 
     there(0)
+    own = [product(gated, w, 0, d) for d in range(2)]
     for p in range(PARTS):
         at = pl.ds(p * lw, lw)
         arrived(gated_in.at[:, at], rg.at[p], sg.at[p], partner)
     both = (ahead, behind)
+    chunk = tok // CHUNKS
     for d in range(2):
-        relay_out[d] = partial(0, d).astype(BF16)
-        sends.append(send(relay_out.at[d], relay_in.at[d], sr.at[d], rr.at[d], both[d]))
+        relay_out[d] = (own[d] + product(gated_in, w_in, 0, d)).astype(BF16)
+        for r in range(CHUNKS):
+            at = pl.ds(r * chunk, chunk)
+            sends.append(send(relay_out.at[d, at], relay_in.at[d, at], sr.at[d, r], rr.at[d, r], both[d]))
     for d in range(2):
         there(1 + d)
-        chip_out[d, 1 - d] = partial(1 + d, 1 - d).astype(BF16)
-        sends.append(send(chip_out.at[d, 1 - d], chip_in.at[d, 1 - d], sx.at[d, 1 - d], rx.at[d, 1 - d], both[d]))
-    for d in range(2):
-        term = partial(1 + d, d)
-        arrived(relay_in.at[d], rr.at[d], sr.at[d], both[1 - d])
-        chip_out[d, d] = (term + relay_in[d].astype(F32)).astype(BF16)
-        sends.append(send(chip_out.at[d, d], chip_in.at[d, d], sx.at[d, d], rx.at[d, d], both[d]))
+        direct_out[d] = partial(1 + d, 1 - d).astype(BF16)
+        sends.append(send(direct_out.at[d], direct_in.at[d], sd.at[d], rd.at[d], both[d]))
+    terms = [partial(1 + d, d) for d in range(2)]
+    for r in range(CHUNKS):
+        at = pl.ds(r * chunk, chunk)
+        for d in range(2):
+            arrived(relay_in.at[d, at], rr.at[d, r], sr.at[d, r], both[1 - d])
+            rows_of = slice(r * chunk, (r + 1) * chunk)
+            chip_out[d, rows_of] = (terms[d][rows_of] + relay_in[d, rows_of].astype(F32)).astype(BF16)
+            sends.append(send(chip_out.at[d, at], chip_in.at[d, at], sx.at[d, r], rx.at[d, r], both[d]))
     there(3)
     own = [partial(3, part) for part in range(2)]
     for d in range(2):
-        arrived(chip_in.at[d, 1 - d], rx.at[d, 1 - d], sx.at[d, 1 - d], both[1 - d])
-        own[1 - d] = own[1 - d] + chip_in[d, 1 - d].astype(F32)
-    for d in range(2):
-        arrived(chip_in.at[d, d], rx.at[d, d], sx.at[d, d], both[1 - d])
-        out_ref[:, d * half:(d + 1) * half] = (own[d] + chip_in[d, d].astype(F32)).astype(BF16)
+        arrived(direct_in.at[d], rd.at[d], sd.at[d], both[1 - d])
+        own[1 - d] = own[1 - d] + direct_in[d].astype(F32)
+    for r in range(CHUNKS):
+        at = pl.ds(r * chunk, chunk)
+        rows_of = slice(r * chunk, (r + 1) * chunk)
+        for d in range(2):
+            arrived(chip_in.at[d, at], rx.at[d, r], sx.at[d, r], both[1 - d])
+            out_ref[rows_of, d * half:(d + 1) * half] = (own[d][rows_of] + chip_in[d, rows_of].astype(F32)).astype(BF16)
 
     for copy in sends:
         copy.wait_send()
@@ -207,6 +219,7 @@
         sl, lw = DH // nz, feat // PARTS
         dma = pltpu.SemaphoreType.DMA
         slices = pltpu.VMEM((PARTS, nz, sl, lw), BF16)
+        halves = pltpu.VMEM((2, tok, width // 2), BF16)
         return pl.pallas_call(
             functools.partial(kernel, ny, nz, nx),
             out_shape=jax.ShapeDtypeStruct((tok, width), BF16),
@@ -219,11 +232,10 @@
                 slices, slices, pltpu.VMEM((PARTS, nz, sl, lw), F32), pltpu.VMEM((PARTS, sl, lw), BF16),
                 pltpu.VMEM((PARTS, ny, sl, lw), BF16), slices, slices,
                 pltpu.VMEM((tok, feat), F32), pltpu.VMEM((tok, feat), BF16), pltpu.VMEM((tok, feat), BF16),
-                pltpu.VMEM((2, tok, width // 2), BF16), pltpu.VMEM((2, tok, width // 2), BF16),
-                pltpu.VMEM((2, 2, tok, width // 2), BF16), pltpu.VMEM((2, 2, tok, width // 2), BF16),
+                halves, halves, halves, halves, halves, halves,
                 dma((5,)), dma((nx,)), dma((PARTS, nz)), dma((PARTS, nz)), dma((PARTS, ny)), dma((PARTS, ny)),
                 dma((PARTS, nz)), dma((PARTS, nz)), dma((nx,)), dma((nx,)), dma((PARTS,)), dma((PARTS,)),
-                dma((2,)), dma((2,)), dma((2, 2)), dma((2, 2)),
+                dma((2, CHUNKS)), dma((2, CHUNKS)), dma((2,)), dma((2,)), dma((2, CHUNKS)), dma((2, CHUNKS)),
             ],
             compiler_params=pltpu.CompilerParams(collective_id=0, has_side_effects=True),
         )(query_rows, key_rows, value_rows, block_mask, norm_gain.reshape(1, feat), out_weight)

time: 39.5 us -> 39.3 us (level)
  the two profiles are of different devices: /device:TPU:41 before, /device:TPU:49 now
where the time goes in v3:
time: 39.3 us; the launch traced here: 39.1 us
  Pallas kernels  36.9 us (94%)
  local copies, waits for them, and re-layouts  1.57 us (4%)
  between operations  0.66 us (2%)
    pallas_call x1, Pallas kernels, local(): pl.pallas_call(functools.partial(kernel, ny, nz, nx), out_shape=jax.Shape...  36.9 us
    unnamed x1, local copies, waits for them, and re-layouts  1.57 us

profile of v3, /device:TPU:49, one launch (start us, length us, event | category | flops | bytes accessed | tf_op | source)
XLA Modules:
  0.0 39.1 jit_solution(13056290600436953187)
XLA Ops:
  0.7 36.9 %shard_map.64 = bf16[128,512]{1,0:T(8,128)(2,1)} custom-call(bf16[128,512]{1,0:T(8,128)(2,1)} %q_hbm.1, bf16[128,512]{1,0:T(8,128)(2,1)} %k_hbm.1, bf16[128,512]{1,0:T(8,128)(2,1)} %v_hbm.1, s32[1,1]{1,0:T(1,128)S(6)} %copy.8.m_hbm, f32[1,512]{1,0:T(1,128)} %bitcast.1, bf16[512,4096]{1,0:T(8,128)(2,1)} %w_hbm.1), custom_call_target="tpu_custom_call" | custom-call | tf_op jit(solution)/shard_map/pallas_call | solution.py:223
  37.5 1.6 %copy.9 = bf16[128,512]{1,0:T(8,128)(2,1)} copy(bf16[128,512]{1,0:T(8,128)(2,1)} %shard_map.64) | data formatting | bytes 262144

commit v4 on v3

--- a/solution.py
+++ b/solution.py
@@ -93,8 +93,6 @@
         for j in far_first(nz):
             pz, device = row_peer(j)
             sends.append(send(state.at[p, pz], rows.at[p, z], sa.at[p, j], ra.at[p, z], device))
-    for i in range(nx):
-        sends.append(send(block(i, 1 - c), w_in.at[i], sw.at[i], rw.at[i], partner))
     for p in range(PARTS):
         rows[p, z] = state[p, z]
 
@@ -123,6 +121,8 @@
             def _():
                 send(total.at[p], cols.at[p, y], sb.at[p, j], rb.at[p, y], ((y + j) * nz + z, ten))
 
+    for i in range(nx):
+        sends.append(send(block(i, 1 - c), w_in.at[i], sw.at[i], rw.at[i], partner))
     for p in range(PARTS):
         for j in range(1, ny):
             @pl.when(y - j >= 0)

time: 39.3 us -> 39.3 us (level)
  no operation moved by 1% of the time
where the time goes in v4:
time: 39.3 us; the launch traced here: 39.1 us
  Pallas kernels  36.9 us (94%)
  local copies, waits for them, and re-layouts  1.57 us (4%)
  between operations  0.66 us (2%)
    pallas_call x1, Pallas kernels, local(): pl.pallas_call(functools.partial(kernel, ny, nz, nx), out_shape=jax.Shape...  36.9 us
    unnamed x1, local copies, waits for them, and re-layouts  1.57 us

profile of v4, /device:TPU:49, one launch (start us, length us, event | category | flops | bytes accessed | tf_op | source)
XLA Modules:
  0.0 39.1 jit_solution(14668612230847909753)
XLA Ops:
  0.7 36.9 %shard_map.64 = bf16[128,512]{1,0:T(8,128)(2,1)} custom-call(bf16[128,512]{1,0:T(8,128)(2,1)} %q_hbm.1, bf16[128,512]{1,0:T(8,128)(2,1)} %k_hbm.1, bf16[128,512]{1,0:T(8,128)(2,1)} %v_hbm.1, s32[1,1]{1,0:T(1,128)S(6)} %copy.8.m_hbm, f32[1,512]{1,0:T(1,128)} %bitcast.1, bf16[512,4096]{1,0:T(8,128)(2,1)} %w_hbm.1), custom_call_target="tpu_custom_call" | custom-call | tf_op jit(solution)/shard_map/pallas_call | solution.py:223
  37.5 1.6 %copy.9 = bf16[128,512]{1,0:T(8,128)(2,1)} copy(bf16[128,512]{1,0:T(8,128)(2,1)} %shard_map.64) | data formatting | bytes 262144
